TPU v7x, 32 devices: a whole 2x2x4 slice. The times are simulated.
32 devices in a mesh: dp: 8 (over y, x, core), blk: 4 (over z).
Axes of the slice: x: 2, y: 2, z: 4, core: 2. Of those that a mesh axis runs over, the one named last changes fastest.
Arguments:
- tokens: bfloat16 [24, 1024, 1024], P('dp', 'blk'), may hold values from -6 to 6
- cotangent: bfloat16 [24, 1024, 1024], P('dp', 'blk'), may hold values from -6 to 6
- domain_ids: int32 [24, 1024], P('dp', 'blk'), may hold values from 0 to 21
- domain_weight: float32 [22], replicated, may hold values from 0.3 to 3
- frozen_input_weights: bfloat16 [1024, 8192], P('dp'), may hold values from -0.1875 to 0.1875
- bias_in: bfloat16 [8192], replicated, may hold values from -1.25 to 1.25
- frozen_down_weight: bfloat16 [4096, 1024], P('dp'), may hold values from -0.09375 to 0.09375
- bias_ff: bfloat16 [1024], replicated, may hold values from -1.25 to 1.25
- norm_gain: float32 [2, 1024], replicated, may hold values from 0.5 to 1.5
- norm_shift: float32 [2, 1024], replicated, may hold values from -1.25 to 1.25
- adapt_a: float32 [1024, 384], P('dp'), may hold values from -0.1875 to 0.1875
- adapt_a_ff: float32 [4096, 128], P('dp'), may hold values from -0.09375 to 0.09375
- adapt_b: float32 [128, 8192], P(None, 'dp'), may hold values from -0.5 to 0.5
- adapt_b_ff: float32 [128, 1024], P(None, 'dp'), may hold values from -0.5 to 0.5
- mean_a: float32 [1024, 384], P('dp'), may hold values from -192 to 192
- mean_a_ff: float32 [4096, 128], P('dp'), may hold values from -192 to 192
- mean_b: float32 [128, 8192], P(None, 'dp'), may hold values from -192 to 192
- mean_b_ff: float32 [128, 1024], P(None, 'dp'), may hold values from -192 to 192
- square_a: float32 [1024, 384], P('dp'), may hold values from 100 to 100000
- square_a_ff: float32 [4096, 128], P('dp'), may hold values from 100 to 100000
- square_b: float32 [128, 8192], P(None, 'dp'), may hold values from 100 to 100000
- square_b_ff: float32 [128, 1024], P(None, 'dp'), may hold values from 100 to 100000
- keep_a: int32 [1024, 384], P('dp'), may hold values 0 or 1
- keep_a_ff: int32 [4096, 128], P('dp'), may hold values 0 or 1
- keep_b: int32 [128, 8192], P(None, 'dp'), may hold values 0 or 1
- keep_b_ff: int32 [128, 1024], P(None, 'dp'), may hold values 0 or 1
Outputs:
- mixed: bfloat16 [24, 1024, 1024], P('dp', 'blk')
- grad_tokens: bfloat16 [24, 1024, 1024], P('dp', 'blk')
- grad_gain: float32 [2, 1024], replicated
- grad_shift: float32 [2, 1024], replicated
- grad_a: float32 [1024, 384], P('dp')
- grad_a_ff: float32 [4096, 128], P('dp')
- grad_b: float32 [128, 8192], P(None, 'dp')
- grad_b_ff: float32 [128, 1024], P(None, 'dp')
- new_mean_a: float32 [1024, 384], P('dp')
- new_square_a: float32 [1024, 384], P('dp')
- new_mean_a_ff: float32 [4096, 128], P('dp')
- new_square_a_ff: float32 [4096, 128], P('dp')
- new_mean_b: float32 [128, 8192], P(None, 'dp')
- new_square_b: float32 [128, 8192], P(None, 'dp')
- new_mean_b_ff: float32 [128, 1024], P(None, 'dp')
- new_square_b_ff: float32 [128, 1024], P(None, 'dp')
- folded_input_weights: bfloat16 [1024, 8192], P('dp')
- folded_down_weight: bfloat16 [4096, 1024], P('dp')
All inputs are finite; a program needn't handle non-finite values. No bound on the sum of `keep_a` or of `keep_a_ff` or of `keep_b` or of `keep_b_ff` on one device may be relied on, other than what follows from the above.
Results may differ from a plain program's by a relative error of at most 0.025.
Values may be sent and summed in bfloat16 or wider, within the bound.
A program may use at most 320 MiB of HBM per device.

v0:
```python
import math
import jax
import jax.numpy as jnp
from jax import lax
from jax.sharding import PartitionSpec as P

HEADS = 16
ROTARY = 16
DOMAINS = 22
highest = lax.Precision.HIGHEST
adapter_scale = 0.25
rope_base = 10000.0
norm_eps = 1e-05
masked_score = -1e30
first_fix = 1.0 - (0.9**10) ** 10
second_fix = 1.0 - (0.999**10) ** 10


def matrix_product(left, right):
    return jnp.dot(left, right, preferred_element_type=jnp.float32)


def product_right_transposed(left, right):
    return lax.dot_general(
        left, right, (((1,), (1,)), ((), ())), preferred_element_type=jnp.float32
    )


def product_left_transposed(left, right):
    return lax.dot_general(
        left, right, (((0,), (0,)), ((), ())), preferred_element_type=jnp.float32
    )


def precise_product(left, right):
    return jnp.dot(left, right, precision=highest)


def layer_norm(values, gain, shift):
    centre = values - jnp.mean(values, axis=-1, keepdims=True)
    spread = jnp.mean(centre * centre, axis=-1, keepdims=True)
    return centre * lax.rsqrt(spread + norm_eps) * gain + shift


def exact_gelu(values):
    return jax.nn.gelu(values, approximate=False)


def rope_tables(positions, rotary):
    half = rotary // 2
    freqs = rope_base ** (-(jnp.arange(half, dtype=jnp.float32) * 2.0) / rotary)
    angles = positions.astype(jnp.float32)[:, None] * freqs[None, :]
    return (jnp.cos(angles), jnp.sin(angles))


def rotate(values, cosine, sine, rotary):
    half = rotary // 2
    front = values[..., :half]
    back = values[..., half:rotary]
    rest = values[..., rotary:]
    cos_b = cosine[:, None, :]
    sin_b = sine[:, None, :]
    return jnp.concatenate(
        [front * cos_b - back * sin_b, back * cos_b + front * sin_b, rest], axis=-1
    )


def project(input_rows, weight_matrix, bias_vector, down, upper_factor):
    middle_rows = matrix_product(input_rows, down).astype(jnp.bfloat16)
    return (
        matrix_product(input_rows, weight_matrix)
        + bias_vector.astype(jnp.float32)
        + adapter_scale * matrix_product(middle_rows, upper_factor),
        middle_rows,
    )


def project_back(
    output_gradient, input_rows, middle_rows, weight_matrix, bias_vector, down, upper_factor
):
    middle_gradient = (
        adapter_scale * product_right_transposed(output_gradient, upper_factor)
    ).astype(jnp.bfloat16)
    upper_gradient = adapter_scale * product_left_transposed(middle_rows, output_gradient)
    grad_down = product_left_transposed(input_rows, middle_gradient)
    grad_in = product_right_transposed(output_gradient, weight_matrix) + product_right_transposed(
        middle_gradient, down
    )
    return (grad_in, grad_down, upper_gradient)


def split_blocks(full, bias_in, bias_ff, width, rank):
    w_all, w_ff, a_all, a_ff, b_all, b_ff = full
    part_qkv = (w_all[:, : 3 * width], bias_in[: 3 * width], a_all[:, :rank], b_all[:, : 3 * width])
    part_att = (
        w_all[:, 3 * width : 4 * width],
        bias_in[3 * width : 4 * width],
        a_all[:, rank : 2 * rank],
        b_all[:, 3 * width : 4 * width],
    )
    part_up = (
        w_all[:, 4 * width :],
        bias_in[4 * width :],
        a_all[:, 2 * rank :],
        b_all[:, 4 * width :],
    )
    part_ff = (w_ff, bias_ff, a_ff, b_ff)
    return (part_qkv, part_att, part_up, part_ff)


def adam_update(param, grad, mean, square, keep):
    mean_new = 0.9 * mean + 0.1 * grad
    square_new = 0.999 * square + 0.001 * grad * grad
    fresh = param - 0.01 * (mean_new / first_fix) / (jnp.sqrt(square_new / second_fix) + 1e-08)
    kept = keep.astype(jnp.float32)
    return (fresh, mean_new * kept, square_new * kept)


def body(
    tokens,
    cotangent,
    domain_ids,
    domain_weight,
    frozen_input_weights,
    bias_in,
    frozen_down_weight,
    bias_ff,
    norm_gain,
    norm_shift,
    adapt_a,
    adapt_a_ff,
    adapt_b,
    adapt_b_ff,
    mean_a,
    mean_a_ff,
    mean_b,
    mean_b_ff,
    square_a,
    square_a_ff,
    square_b,
    square_b_ff,
    keep_a,
    keep_a_ff,
    keep_b,
    keep_b_ff,
):
    seqs, span, width = tokens.shape
    rows = seqs * span
    rank = adapt_b.shape[0]
    depth = width // HEADS
    att_scale = 1.0 / math.sqrt(depth)
    shards = (
        frozen_input_weights,
        frozen_down_weight,
        adapt_a.astype(jnp.bfloat16),
        adapt_a_ff.astype(jnp.bfloat16),
        adapt_b.astype(jnp.bfloat16),
        adapt_b_ff.astype(jnp.bfloat16),
    )
    whole = (
        lax.all_gather(shards[0], "dp", axis=0, tiled=True),
        lax.all_gather(shards[1], "dp", axis=0, tiled=True),
        lax.all_gather(shards[2], "dp", axis=0, tiled=True),
        lax.all_gather(shards[3], "dp", axis=0, tiled=True),
        lax.all_gather(shards[4], "dp", axis=1, tiled=True),
        lax.all_gather(shards[5], "dp", axis=1, tiled=True),
    )
    part_qkv, part_att, part_up, part_ff = split_blocks(whole, bias_in, bias_ff, width, rank)
    input_rows = tokens.astype(jnp.float32).reshape(rows, width)
    first_f, first_pull = jax.vjp(layer_norm, input_rows, norm_gain[0], norm_shift[0])
    second_f, second_pull = jax.vjp(layer_norm, input_rows, norm_gain[1], norm_shift[1])
    first = first_f.astype(jnp.bfloat16)
    second = second_f.astype(jnp.bfloat16)
    joint, middle_qkv = project(first, *part_qkv)
    joint3 = joint.reshape(seqs, span, 3 * width)
    positions = lax.axis_index("blk") * span + jnp.arange(span, dtype=jnp.int32)
    cosine, sine = rope_tables(positions, ROTARY)

    def turn(query_raw, key_raw):
        return (rotate(query_raw, cosine, sine, ROTARY), rotate(key_raw, cosine, sine, ROTARY))

    (query_r, key_r), rope_pull = jax.vjp(
        turn,
        joint3[..., :width].reshape(seqs, span, HEADS, depth),
        joint3[..., width : 2 * width].reshape(seqs, span, HEADS, depth),
    )
    query_b = query_r.astype(jnp.bfloat16)
    key_local = key_r.astype(jnp.bfloat16)
    value_local = joint3[..., 2 * width :].reshape(seqs, span, HEADS, depth).astype(jnp.bfloat16)
    key_send = key_local.reshape(seqs, span, width)
    value_send = value_local.reshape(seqs, span, width)
    top = jnp.full((seqs, HEADS, span), masked_score, jnp.float32)
    key_piece = lax.all_gather(key_send, "blk", axis=1, tiled=True)
    value_piece = lax.all_gather(value_send, "blk", axis=1, tiled=True)
    count = key_piece.shape[1]
    key_h = key_piece.reshape(seqs, count, HEADS, depth)
    value_h = value_piece.reshape(seqs, count, HEADS, depth)
    scores = (
        jnp.einsum("sqhe,skhe->shqk", query_b, key_h, preferred_element_type=jnp.float32)
        * att_scale
    )
    allowed = positions[:, None] >= jnp.arange(count, dtype=jnp.int32)[None, :]
    scores = jnp.where(allowed, scores, masked_score)
    new_top = jnp.maximum(top, jnp.max(scores, axis=-1))
    weights = jnp.where(allowed, jnp.exp(scores - new_top[..., None]), 0.0)
    total = jnp.sum(weights, axis=-1)
    update = jnp.einsum(
        "shqk,skhe->sqhe", weights.astype(jnp.bfloat16), value_h, preferred_element_type=jnp.float32
    )
    accum = update
    top, total, accum = (new_top, total, accum)
    attended_f = (accum / jnp.transpose(total, (0, 2, 1))[..., None]).reshape(rows, width)
    log_total = top + jnp.log(total)
    attended = attended_f.astype(jnp.bfloat16)
    branch_att, middle_att = project(attended, *part_att)
    up_pre, middle_up = project(second, *part_up)
    hidden_f, gelu_pull = jax.vjp(exact_gelu, up_pre)
    hidden = hidden_f.astype(jnp.bfloat16)
    branch_ff, middle_ff = project(hidden, *part_ff)
    mixed = (input_rows + branch_att + branch_ff).astype(jnp.bfloat16).reshape(seqs, span, width)
    lookup = (domain_ids[..., None] == jnp.arange(DOMAINS, dtype=jnp.int32)).astype(jnp.float32)
    row_weight = jnp.sum(lookup * domain_weight, axis=-1).reshape(rows, 1)
    row_grad = cotangent.astype(jnp.float32).reshape(rows, width) * row_weight
    grad_low = row_grad.astype(jnp.bfloat16)
    grad_hidden, grad_a_ffp, grad_b_ffp = project_back(grad_low, hidden, middle_ff, *part_ff)
    upper_gradient = gelu_pull(grad_hidden)[0].astype(jnp.bfloat16)
    grad_second, grad_a_up, grad_b_up = project_back(upper_gradient, second, middle_up, *part_up)
    grad_att_f, grad_a_att, grad_b_att = project_back(grad_low, attended, middle_att, *part_att)
    grad_att = grad_att_f.astype(jnp.bfloat16)
    grad_heads = grad_att.reshape(seqs, span, HEADS, depth)
    delta = jnp.transpose(
        jnp.sum(
            grad_heads.astype(jnp.float32) * attended_f.reshape(seqs, span, HEADS, depth), axis=-1
        ),
        (0, 2, 1),
    )
    key_piece = lax.all_gather(key_send, "blk", axis=1, tiled=True)
    value_piece = lax.all_gather(value_send, "blk", axis=1, tiled=True)
    count = key_piece.shape[1]
    key_h = key_piece.reshape(seqs, count, HEADS, depth)
    value_h = value_piece.reshape(seqs, count, HEADS, depth)
    scores = (
        jnp.einsum("sqhe,skhe->shqk", query_b, key_h, preferred_element_type=jnp.float32)
        * att_scale
    )
    allowed = positions[:, None] >= jnp.arange(count, dtype=jnp.int32)[None, :]
    weights = jnp.where(allowed, jnp.exp(scores - log_total[..., None]), 0.0)
    grad_w = jnp.einsum("sqhe,skhe->shqk", grad_heads, value_h, preferred_element_type=jnp.float32)
    grad_s = (weights * (grad_w - delta[..., None])).astype(jnp.bfloat16)
    grad_query = (
        jnp.einsum("shqk,skhe->sqhe", grad_s, key_h, preferred_element_type=jnp.float32) * att_scale
    )
    stats_lse, stats_delta = (
        lax.all_gather(log_total.astype(jnp.bfloat16), "blk", axis=2, tiled=True).astype(
            log_total.dtype
        ),
        lax.all_gather(delta.astype(jnp.bfloat16), "blk", axis=2, tiled=True).astype(delta.dtype),
    )
    query_piece = lax.all_gather(query_b.reshape(seqs, span, width), "blk", axis=1, tiled=True)
    grad_piece = lax.all_gather(grad_att.reshape(seqs, span, width), "blk", axis=1, tiled=True)
    count = query_piece.shape[1]
    query_h = query_piece.reshape(seqs, count, HEADS, depth)
    grad_h = grad_piece.reshape(seqs, count, HEADS, depth)
    scores = (
        jnp.einsum("sqhe,skhe->shqk", query_h, key_local, preferred_element_type=jnp.float32)
        * att_scale
    )
    allowed = jnp.arange(count, dtype=jnp.int32)[:, None] >= positions[None, :]
    weights = jnp.where(allowed, jnp.exp(scores - stats_lse[..., None]), 0.0)
    grad_v = jnp.einsum(
        "shqk,sqhe->skhe", weights.astype(jnp.bfloat16), grad_h, preferred_element_type=jnp.float32
    )
    grad_w = jnp.einsum("sqhe,skhe->shqk", grad_h, value_local, preferred_element_type=jnp.float32)
    grad_s = (weights * (grad_w - stats_delta[..., None])).astype(jnp.bfloat16)
    grad_k = (
        jnp.einsum("shqk,sqhe->skhe", grad_s, query_h, preferred_element_type=jnp.float32)
        * att_scale
    )
    grad_query_raw, grad_key_raw = rope_pull((grad_query, grad_k))
    grad_joint = jnp.concatenate(
        [
            grad_query_raw.reshape(rows, width),
            grad_key_raw.reshape(rows, width),
            grad_v.reshape(rows, width),
        ],
        axis=1,
    ).astype(jnp.bfloat16)
    grad_first, grad_a_qkv, grad_b_qkv = project_back(grad_joint, first, middle_qkv, *part_qkv)
    back_one = first_pull(grad_first)
    back_two = second_pull(grad_second)
    grad_tokens = (
        (row_grad + back_one[0] + back_two[0]).astype(jnp.bfloat16).reshape(seqs, span, width)
    )
    gain_part = jnp.stack([back_one[1], back_two[1]])
    shift_part = jnp.stack([back_one[2], back_two[2]])
    grad_a_part = jnp.concatenate([grad_a_qkv, grad_a_att, grad_a_up], axis=1)
    grad_b_part = jnp.concatenate([grad_b_qkv, grad_b_att, grad_b_up], axis=1)
    summed = lax.psum(
        (grad_a_part, grad_a_ffp, grad_b_part, grad_b_ffp, gain_part, shift_part), ("dp", "blk")
    )
    owner = lax.axis_index("dp")
    grad_a = lax.dynamic_slice_in_dim(summed[0], owner * adapt_a.shape[0], adapt_a.shape[0], 0)
    grad_a_ff = lax.dynamic_slice_in_dim(
        summed[1], owner * adapt_a_ff.shape[0], adapt_a_ff.shape[0], 0
    )
    grad_b = lax.dynamic_slice_in_dim(summed[2], owner * adapt_b.shape[1], adapt_b.shape[1], 1)
    grad_b_ff = lax.dynamic_slice_in_dim(
        summed[3], owner * adapt_b_ff.shape[1], adapt_b_ff.shape[1], 1
    )
    grad_gain = summed[4]
    grad_shift = summed[5]
    fresh_a, new_mean_a, new_square_a = adam_update(adapt_a, grad_a, mean_a, square_a, keep_a)
    reset_down_adapter_left, new_mean_a_ff, new_square_a_ff = adam_update(
        adapt_a_ff, grad_a_ff, mean_a_ff, square_a_ff, keep_a_ff
    )
    fresh_b, new_mean_b, new_square_b = adam_update(adapt_b, grad_b, mean_b, square_b, keep_b)
    reset_down_adapter_right, new_mean_b_ff, new_square_b_ff = adam_update(
        adapt_b_ff, grad_b_ff, mean_b_ff, square_b_ff, keep_b_ff
    )
    fresh_b_all, reset_down_right_stacked = (
        lax.all_gather(fresh_b.astype(jnp.bfloat16), "dp", axis=1, tiled=True).astype(
            fresh_b.dtype
        ),
        lax.all_gather(
            reset_down_adapter_right.astype(jnp.bfloat16), "dp", axis=1, tiled=True
        ).astype(reset_down_adapter_right.dtype),
    )
    input_weight_update = jnp.concatenate(
        [
            precise_product(fresh_a[:, :rank], fresh_b_all[:, : 3 * width]),
            precise_product(fresh_a[:, rank : 2 * rank], fresh_b_all[:, 3 * width : 4 * width]),
            precise_product(fresh_a[:, 2 * rank :], fresh_b_all[:, 4 * width :]),
        ],
        axis=1,
    )
    folded_input_weights = (
        frozen_input_weights.astype(jnp.float32) + adapter_scale * input_weight_update
    ).astype(jnp.bfloat16)
    folded_down_weight = (
        frozen_down_weight.astype(jnp.float32)
        + adapter_scale * precise_product(reset_down_adapter_left, reset_down_right_stacked)
    ).astype(jnp.bfloat16)
    return (
        mixed,
        grad_tokens,
        grad_gain,
        grad_shift,
        grad_a,
        grad_a_ff,
        grad_b,
        grad_b_ff,
        new_mean_a,
        new_square_a,
        new_mean_a_ff,
        new_square_a_ff,
        new_mean_b,
        new_square_b,
        new_mean_b_ff,
        new_square_b_ff,
        folded_input_weights,
        folded_down_weight,
    )


def solution(mesh):
    in_specs = (
        P("dp", "blk", None),
        P("dp", "blk", None),
        P("dp", "blk"),
        P(),
        P("dp", None),
        P(),
        P("dp", None),
        P(),
        P(),
        P(),
        P("dp", None),
        P("dp", None),
        P(None, "dp"),
        P(None, "dp"),
        P("dp", None),
        P("dp", None),
        P(None, "dp"),
        P(None, "dp"),
        P("dp", None),
        P("dp", None),
        P(None, "dp"),
        P(None, "dp"),
        P("dp", None),
        P("dp", None),
        P(None, "dp"),
        P(None, "dp"),
    )
    out_specs = (
        P("dp", "blk", None),
        P("dp", "blk", None),
        P(),
        P(),
        P("dp", None),
        P("dp", None),
        P(None, "dp"),
        P(None, "dp"),
        P("dp", None),
        P("dp", None),
        P("dp", None),
        P("dp", None),
        P(None, "dp"),
        P(None, "dp"),
        P(None, "dp"),
        P(None, "dp"),
        P("dp", None),
        P("dp", None),
    )
    return jax.shard_map(body, mesh=mesh, in_specs=in_specs, out_specs=out_specs, check_vma=False)
```

profile of v0, /device:TPU:0, one launch (start us, length us, event | category | flops | bytes accessed | tf_op | source)
XLA Modules:
  0.0 990.2 jit_solution(3469510999970349865)
XLA Ops:
  12.5 12.9 %all_gather.45 = bf16[1024,384]{1,0:T(8,128)(2,1)} all-gather(bf16[128,384]{1,0:T(8,128)(2,1)S(1)} %convert_element_type.174), channel_id=1, replica_groups=mesh['dp'=8,'blk'=4] {'dp'}, dimensions={0}, use_global_device_ids=true | all-gather | bytes 884736 | tf_op jit(solution)/shard_map/all_gather | solution.py:163
  30.0 72.5 %all-gather.10.cloned.1.call-done = bf16[1024,8192]{1,0:T(8,128)(2,1)} async-done(((bf16[128,8192]{1,0:T(8,128)(2,1)}), bf16[1024,8192]{1,0:T(8,128)(2,1)}) %all-gather.10.cloned.1.call-update) | async-done | bytes 16777232 | tf_op jit(solution)/shard_map/all_gather | solution.py:161
  102.5 10.2 %fusion.23 = f32[768,3072]{1,0:T(8,128)} fusion(bf16[768,1024]{1,0:T(8,128)(2,1)S(1)} %get-tuple-element.112, bf16[1024,8192]{1,0:T(8,128)(2,1)} %all-gather.10.cloned.1.call-done), kind=kOutput, calls=%fused_computation.39 | convolution fusion | flops 4831838208 | bytes 17301504 | tf_op jit(solution)/shard_map/dot_general | solution.py:20
  112.8 20.2 %all-gather.12.cloned.1.call-done = bf16[128,8192]{1,0:T(8,128)(2,1)} async-done(((bf16[128,1024]{1,0:T(8,128)(2,1)}), bf16[128,8192]{1,0:T(8,128)(2,1)}) %all-gather.12.cloned.1.call-update) | async-done | bytes 2097168 | tf_op jit(solution)/shard_map/all_gather | solution.py:165
  132.9 5.3 multiply_add_fusion.1
  138.3 2.7 fusion.131
  143.1 3.9 copy.73
  147.0 2.4 copy.74
  168.0 10.3 %all_gather.51 = bf16[128,1024]{1,0:T(8,128)(2,1)S(1)} all-gather(bf16[128,128]{1,0:T(8,128)(2,1)} %convert_element_type.194), channel_id=1, replica_groups=mesh['dp'=8,'blk'=4] {'dp'}, dimensions={1}, use_global_device_ids=true | all-gather | bytes 294912 | tf_op jit(solution)/shard_map/all_gather | solution.py:166
  190.3 12.6 %fusion.136 = f32[768,4096]{1,0:T(8,128)} fusion(bf16[768,1024]{1,0:T(8,128)(2,1)S(1)} %fusion.28, bf16[4096,1024]{1,0:T(8,128)(2,1)} %all-gather.18.cloned.1.call-done), kind=kOutput, calls=%fused_computation.232 | convolution fusion | flops 6442450944 | bytes 22544384 | tf_op jit(solution)/shard_map/dot_general | solution.py:24
  202.9 2.8 slice.131
  205.7 3.4 fusion.57
  210.7 3.3 reshape.291
  214.0 5.0 copy.77
  219.0 2.8 maximum_convert_fusion
  222.1 9.4 fusion.19
  231.5 31.8 %multiply_convert_fusion.2 = (bf16[768,4096]{1,0:T(8,128)(2,1)}, f32[768,4096]{1,0:T(8,128)}, f32[768,4096]{1,0:T(8,128)}) fusion(bf16[768,128]{1,0:T(8,128)(2,1)S(1)} %copy-done.54, bf16[128,8192]{1,0:T(8,128)(2,1)S(1)} %copy-done.56, f32[768,4096]{1,0:T(8,128)S(1)} %fusion.19, f32[4096]{0:T(1024)S(1)} %copy-done.84), kind=kOutput, calls=%fused_computation.15 | convolution fusion | flops 1019215872 | bytes 45301760 | tf_op jit(solution)/shard_map/dot_general | solution.py:20
  263.4 17.3 %add_convert_fusion = bf16[768,4096]{1,0:T(8,128)(2,1)} fusion(f32[768,4096]{1,0:T(8,128)} %get-tuple-element.99, f32[768,4096]{1,0:T(8,128)} %fusion.136, f32[768,4096]{1,0:T(8,128)} %get-tuple-element.136, bf16[768,128]{1,0:T(8,128)(2,1)} %fusion.69, bf16[4096,128]{1,0:T(8,128)(2,1)} %all-gather.20.cloned.1.call-done), kind=kOutput, calls=%fused_computation.14 | convolution fusion | flops 852492288 | bytes 45285376 | tf_op jit(solution)/shard_map/dot_general | solution.py:24
  280.7 5.0 fusion.70
  290.0 3.1 fusion.89
  295.5 3.2 fusion.140
  298.8 12.6 %fusion.135 = f32[768,1024]{1,0:T(8,128)} fusion(bf16[768,4096]{1,0:T(8,128)(2,1)} %get-tuple-element.98, bf16[4096,1024]{1,0:T(8,128)(2,1)} %all-gather.18.cloned.1.call-done), kind=kOutput, calls=%fused_computation.231 | convolution fusion | flops 6442450944 | bytes 17825792 | tf_op jit(solution)/shard_map/dot_general | solution.py:20
  311.4 21.1 %all-gather.16.cloned.1.call-done = bf16[3,1024,1024]{1,2,0:T(8,128)(2,1)} async-done(((bf16[3,256,1024]{1,2,0:T(8,128)(2,1)}), bf16[3,1024,1024]{1,2,0:T(8,128)(2,1)}) %all-gather.16.cloned.1.call-update) | async-done | bytes 6291472 | tf_op jit(solution)/shard_map/all_gather | solution.py:193
  332.5 21.8 %select_reduce_fusion = (f32[3,16,256]{2,1,0:T(8,128)S(1)}, f32[3,16,256,1024]{3,2,1,0:T(8,128)}) fusion(pred[256,1024]{1,0:T(8,128)(4,1)S(1)} %copy-done.5, bf16[3,1024,16,64]{1,3,2,0:T(8,128)(2,1)} %bitcast.174, bf16[3,256,16,48]{1,3,2,0:T(8,128)(2,1)S(1)} %copy-done.14, bf16[3,256,16,8]{1,3,2,0:T(8,128)(2,1)S(1)} %get-tuple-element.124, ...), kind=kOutput, calls=%fused_computation.4 | convolution fusion | flops 1653067776 | bytes 58507264 | tf_op jit(solution)/shard_map/sqhe,skhe->shqk/dot_general | solution.py:199
  354.3 23.0 %fusion.1 = f32[3,16,256]{2,1,0:T(8,128)S(1)} fusion(f32[3,16,256,1024]{3,2,1,0:T(8,128)} %get-tuple-element.135, f32[3,16,256]{2,1,0:T(8,128)S(1)} %broadcast_maximum_fusion, pred[256,1024]{1,0:T(8,128)(4,1)S(1)} %copy-done.5), kind=kLoop, calls=%fused_computation.6 | loop fusion | flops 62902272 | bytes 50692096 | tf_op jit(solution)/shard_map/reduce_sum | solution.py:206
  377.3 20.7 %all_gather.53 = bf16[3,16,1024]{2,1,0:T(8,128)(2,1)S(1)} all-gather(bf16[3,16,256]{2,1,0:T(8,128)(2,1)S(1)} %get-tuple-element.96), channel_id=1, replica_groups=mesh['dp'=8,'blk'=4] {'blk'}, dimensions={2}, use_global_device_ids=true | all-gather | bytes 122880 | tf_op jit(solution)/shard_map/all_gather | solution.py:254
  398.0 50.5 %all-gather.14.cloned.1.call-done = bf16[3,1024,1024]{1,2,0:T(8,128)(2,1)} async-done(((bf16[3,256,1024]{1,2,0:T(8,128)(2,1)}), bf16[3,1024,1024]{1,2,0:T(8,128)(2,1)}) %all-gather.14.cloned.1.call-update) | async-done | bytes 6291472 | tf_op jit(solution)/shard_map/all_gather | solution.py:194
  448.5 23.5 %multiply_reduce_fusion = (f32[3,256,16]{1,2,0:T(8,128)S(1)}, bf16[3,256,16,64]{1,3,2,0:T(8,128)(2,1)}) fusion(bf16[3,256,16,64]{1,3,2,0:T(8,128)(2,1)S(1)} %copy-done.39, f32[3,256,16]{1,2,0:T(8,128)S(1)} %bitcast.202, bf16[3,1024,16,64]{1,3,2,0:T(8,128)(2,1)} %bitcast.218, f32[3,16,256,1024]{3,2,1,0:T(8,128)} %get-tuple-element.135, ...), kind=kOutput, calls=%fused_computation.86 | convolution fusion | flops 1677447168 | bytes 60178432 | tf_op jit(solution)/shard_map/shqk,skhe->sqhe/dot_general | solution.py:207
  472.1 28.8 %multiply_bitcast_fusion.1 = f32[3,256,16,64]{1,3,2,0:T(8,128)} fusion(bf16[3,1024,16,64]{1,3,2,0:T(8,128)(2,1)} %bitcast.175, f32[3,16,256,1024]{3,2,1,0:T(8,128)} %get-tuple-element.135, bf16[3,256,16,64]{1,3,2,0:T(8,128)(2,1)S(1)} %copy-done.39, bf16[3,1024,16,64]{1,3,2,0:T(8,128)(2,1)} %bitcast.219, f32[3,16,256]{2,1,0:T(8,128)S(1)} %bitcast.211, ...), kind=kOutput, calls=%fused_computation.85 | convolution fusion | flops 3297509376 | bytes 67993600 | tf_op jit(solution)/shard_map/shqk,skhe->sqhe/dot_general | solution.py:251
  500.9 27.6 %all_gather.55 = bf16[3,16,1024]{2,1,0:T(8,128)(2,1)S(1)} all-gather(bf16[3,16,256]{2,1,0:T(8,128)(2,1)S(1)} %bitcast_convert_fusion), channel_id=1, replica_groups=mesh['dp'=8,'blk'=4] {'blk'}, dimensions={2}, use_global_device_ids=true | all-gather | bytes 122880 | tf_op jit(solution)/shard_map/all_gather | solution.py:257
  529.2 35.5 %all-gather.22.cloned.1.call-done = bf16[3,1024,1024]{1,2,0:T(8,128)(2,1)} async-done(((bf16[3,256,1024]{1,2,0:T(8,128)(2,1)}), bf16[3,1024,1024]{1,2,0:T(8,128)(2,1)}) %all-gather.22.cloned.1.call-update) | async-done | bytes 6291472 | tf_op jit(solution)/shard_map/all_gather | solution.py:259
  564.7 22.0 %fusion.134 = f32[3,16,1024,256]{3,2,1,0:T(8,128)} fusion(bf16[3,1024,16,64]{1,3,2,0:T(8,128)(2,1)} %bitcast.179, bf16[3,256,16,48]{1,3,2,0:T(8,128)(2,1)S(1)} %copy-done.13, bf16[3,256,16,8]{1,3,2,0:T(8,128)(2,1)S(1)} %copy-done.36, bf16[3,256,16,8]{1,3,2,0:T(8,128)(2,1)S(1)} %copy-done.34), kind=kOutput, calls=%fused_computation.230 | convolution fusion | flops 1615331328 | bytes 58195968 | tf_op jit(solution)/shard_map/sqhe,skhe->shqk/dot_general | solution.py:265
  586.7 93.3 %all-gather.24.cloned.1.call-done = bf16[3,1024,1024]{2,1,0:T(8,128)(2,1)} async-done(((bf16[3,256,1024]{2,1,0:T(8,128)(2,1)}), bf16[3,1024,1024]{2,1,0:T(8,128)(2,1)}) %all-gather.24.cloned.1.call-update) | async-done | bytes 6291472 | tf_op jit(solution)/shard_map/all_gather | solution.py:260
  680.1 8.7 copy.80
  688.7 20.5 %fusion.64 = bf16[3,256,16,64]{1,3,2,0:T(8,128)(2,1)} fusion(bf16[3,1024,16,64]{1,3,2,0:T(8,128)(2,1)} %bitcast.189, f32[3,16,1024,256]{3,2,1,0:T(8,128)} %fusion.134, f32[3,16,1024]{2,1,0:T(8,128)S(1)} %convert_element_type.203, pred[1024,256]{1,0:T(8,128)(4,1)S(1)} %copy-done.60), kind=kOutput, calls=%fused_computation.97 | convolution fusion | flops 1661730816 | bytes 58654720 | tf_op jit(solution)/shard_map/shqk,sqhe->skhe/dot_general | solution.py:270
  709.2 28.0 %multiply_bitcast_fusion = f32[3,256,16,64]{1,3,2,0:T(8,128)} fusion(bf16[3,1024,16,64]{1,3,2,0:T(8,128)(2,1)} %bitcast.180, f32[3,16,1024,256]{3,2,1,0:T(8,128)} %fusion.134, bf16[3,1024,16,64]{1,3,2,0:T(8,128)(2,1)} %bitcast.190, bf16[3,256,16,64]{1,3,2,0:T(8,128)(2,1)} %bitcast.191, f32[3,16,1024]{2,1,0:T(8,128)} %convert_element_type.206, ...), kind=kOutput, calls=%fused_computation.83 | convolution fusion | flops 3297509376 | bytes 68288512 | tf_op jit(solution)/shard_map/shqk,sqhe->skhe/dot_general | solution.py:276
  754.6 2.7 fusion.67
  761.6 8.6 fusion.21
  772.9 13.2 %fusion.128 = (f32[1024]{0:T(1024)S(1)}, f32[768]{0:T(1024)S(1)}, f32[768]{0:T(1024)S(1)}, f32[1024]{0:T(1024)S(1)}, f32[768,1024]{1,0:T(8,128)S(1)}) fusion(f32[1024]{0:T(1024)S(1)} %bitcast.208, f32[768]{0:T(1024)S(1)} %copy-done.71, bf16[3,256,1024]{2,1,0:T(8,128)(2,1)S(1)} %copy-done.1, f32[768,1024]{1,0:T(8,128)S(1)} %convolution_add_fusion, ...), kind=kOutput, calls=%fused_computation.225 | convolution fusion | flops 6451097600 | bytes 25715712 | tf_op jit(solution)/shard_map/dot_general | solution.py:24
  786.1 2.9 fusion.44
  789.1 39.3 %all-reduce.6 = (f32[2,1024]{1,0:T(2,128)}, f32[2,1024]{1,0:T(2,128)}) all-reduce(f32[2,1024]{1,0:T(2,128)S(1)} %pad_maximum_fusion.2, f32[2,1024]{1,0:T(2,128)S(1)} %pad_maximum_fusion.3), channel_id=1, replica_groups=mesh['dp'=8,'blk'=4] {'dp','blk'}, use_global_device_ids=true, to_apply=%region_12.13 | all-reduce | flops 4096 | bytes 32768 | tf_op jit(solution)/shard_map/psum | solution.py:298
  828.4 3.1 fusion.93
  831.5 5.1 fusion.59
  836.6 103.6 %all-reduce.10.cloned.1.call-done = (f32[1024,384]{0,1:T(8,128)}, f32[4096,128]{1,0:T(8,128)}, f32[128,8192]{1,0:T(8,128)}, f32[128,1024]{1,0:T(8,128)}) async-done(((f32[1024,384]{0,1:T(8,128)}, f32[4096,128]{1,0:T(8,128)}, f32[128,8192]{1,0:T(8,128)}, f32[128,1024]{1,0:T(8,128)}), (f32[1024,384]{0,1:T(8,128)}, f32[4096,128]{1,0:T(8,128)}, f32[128,8192]{1,0:T(8,128)}, ...) | async-done | bytes 8388624 | tf_op jit(solution)/shard_map/psum | solution.py:298
  940.2 2.6 subtract_convert_fusion
  942.9 6.1 fusion.51
  949.3 3.2 fusion.30
  957.2 10.1 %all_gather.57 = bf16[128,1024]{1,0:T(8,128)(2,1)S(1)} all-gather(bf16[128,128]{1,0:T(8,128)(2,1)S(1)} %get-tuple-element.88), channel_id=1, replica_groups=mesh['dp'=8,'blk'=4] {'dp'}, dimensions={1}, use_global_device_ids=true | all-gather | bytes 294912 | tf_op jit(solution)/shard_map/all_gather | solution.py:324
  (305 shorter events, 96.1 us)
Async XLA Ops:
  7.2 95.3 %all-gather.10.cloned.1.call-start = ((), (), s32[]{:S(2)}) async-start(), calls=%async_computation | async-start | bytes 18874368 | tf_op jit(solution)/shard_map/all_gather | solution.py:161
  8.0 125.0 %all-gather.12.cloned.1.call-start = ((), (), s32[]{:S(2)}) async-start(), calls=%async_computation.1 | async-start | bytes 2359296 | tf_op jit(solution)/shard_map/all_gather | solution.py:165
  9.9 180.5 %all-gather.18.cloned.1.call-start = ((), (), s32[]{:S(2)}) async-start(), calls=%async_computation.4 | async-start | bytes 9437184 | tf_op jit(solution)/shard_map/all_gather | solution.py:162
  10.6 252.8 %all-gather.20.cloned.1.call-start = ((), (), s32[]{:S(2)}) async-start(), calls=%async_computation.5 | async-start | bytes 1179648 | tf_op jit(solution)/shard_map/all_gather | solution.py:164
  11.4 321.1 %all-gather.16.cloned.1.call-start = ((), (), s32[]{:S(2)}) async-start(), calls=%async_computation.3 | async-start | bytes 7864320 | tf_op jit(solution)/shard_map/all_gather | solution.py:193
  12.3 17.6 %copy-start.70 = (f32[768]{0:T(1024)}, f32[768]{0:T(1024)S(1)}, u32[]{:S(2)}) copy-start(f32[768]{0:T(1024)S(1)} %div.87) | copy-start | bytes 9220
  12.3 13.8 %copy-start.80 = (f32[768]{0:T(1024)}, f32[768]{0:T(1024)S(1)}, u32[]{:S(2)}) copy-start(f32[768]{0:T(1024)S(1)} %add.223) | copy-start | bytes 9220
  12.4 17.5 %copy-start.72 = (f32[768]{0:T(1024)}, f32[768]{0:T(1024)S(1)}, u32[]{:S(2)}) copy-start(f32[768]{0:T(1024)S(1)} %rsqrt.13) | copy-start | bytes 9220
  12.4 17.5 %copy-start.74 = (f32[1,1024]{1,0:T(1,128)}, f32[1,1024]{1,0:T(1,128)S(1)}, u32[]{:S(2)}) copy-start(f32[1,1024]{1,0:T(1,128)S(1)} %get-tuple-element.126) | copy-start | bytes 12292
  12.4 17.5 %copy-start.76 = (f32[1,1024]{1,0:T(1,128)}, f32[1,1024]{1,0:T(1,128)S(1)}, u32[]{:S(2)}) copy-start(f32[1,1024]{1,0:T(1,128)S(1)} %get-tuple-element.127) | copy-start | bytes 12292
  28.1 84.6 %copy-start.21 = (bf16[768,1024]{1,0:T(8,128)(2,1)}, bf16[768,1024]{1,0:T(8,128)(2,1)S(1)}, u32[]{:S(2)}) copy-start(bf16[768,1024]{1,0:T(8,128)(2,1)S(1)} %get-tuple-element.112) | copy-start | bytes 4718596
  29.9 103.1 %copy-start.45 = (bf16[768,128]{1,0:T(8,128)(2,1)}, bf16[768,128]{1,0:T(8,128)(2,1)S(1)}, u32[]{:S(2)}) copy-start(bf16[768,128]{1,0:T(8,128)(2,1)S(1)} %convolution_convert_fusion.3) | copy-start | bytes 589828
  30.0 121.2 %copy-start.66 = (f32[256,8]{0,1:T(8,128)}, f32[256,8]{0,1:T(8,128)S(1)}, u32[]{:S(2)}) copy-start(f32[256,8]{0,1:T(8,128)S(1)} %get-tuple-element.132) | copy-start | bytes 24580
  30.0 121.2 %copy-start.68 = (f32[256,8]{0,1:T(8,128)}, f32[256,8]{0,1:T(8,128)S(1)}, u32[]{:S(2)}) copy-start(f32[256,8]{0,1:T(8,128)S(1)} %get-tuple-element.133) | copy-start | bytes 24580
  154.7 293.8 %all-gather.14.cloned.1.call-start = ((), (), s32[]{:S(2)}) async-start(), calls=%async_computation.2 | async-start | bytes 7864320 | tf_op jit(solution)/shard_map/all_gather | solution.py:194
  158.5 24.2 %copy-start.23 = (bf16[768,1024]{1,0:T(8,128)(2,1)S(1)}, bf16[768,1024]{1,0:T(8,128)(2,1)}, u32[]{:S(2)}) copy-start(bf16[768,1024]{1,0:T(8,128)(2,1)} %get-tuple-element.113) | copy-start | bytes 4718596
  158.5 26.3 %copy-start.19 = (bf16[3,256,1024]{2,1,0:T(8,128)(2,1)S(1)}, bf16[3,256,1024]{2,1,0:T(8,128)(2,1)}, u32[]{:S(2)}) copy-start(bf16[3,256,1024]{2,1,0:T(8,128)(2,1)} %param.27) | copy-start | bytes 4718596
  158.6 406.2 %all-gather.22.cloned.1.call-start = ((), (), s32[]{:S(2)}) async-start(), calls=%async_computation.6 | async-start | bytes 7864320 | tf_op jit(solution)/shard_map/all_gather | solution.py:259
  160.6 24.6 %copy-start.78 = (f32[768]{0:T(1024)}, f32[768]{0:T(1024)S(1)}, u32[]{:S(2)}) copy-start(f32[768]{0:T(1024)S(1)} %mul.573) | copy-start | bytes 9220
  185.2 103.5 %copy-start.6 = (bf16[768,1024]{1,0:T(8,128)(2,1)}, bf16[768,1024]{1,0:T(8,128)(2,1)S(1)}, u32[]{:S(2)}) copy-start(bf16[768,1024]{1,0:T(8,128)(2,1)S(1)} %fusion.28) | copy-start | bytes 4718596
  221.8 458.3 %all-gather.24.cloned.1.call-start = ((), (), s32[]{:S(2)}) async-start(), calls=%async_computation.7 | async-start | bytes 7864320 | tf_op jit(solution)/shard_map/all_gather | solution.py:260
  298.7 33.7 %copy-start.5 = (pred[256,1024]{1,0:T(8,128)(4,1)S(1)}, pred[256,1024]{1,0:T(8,128)(4,1)}, u32[]{:S(2)}) copy-start(pred[256,1024]{1,0:T(8,128)(4,1)} %iota_compare_fusion.1) | copy-start | bytes 786436
  298.7 33.7 %copy-start.14 = (bf16[3,256,16,48]{1,3,2,0:T(8,128)(2,1)S(1)}, bf16[3,256,16,48]{1,3,2,0:T(8,128)(2,1)}, u32[]{:S(2)}) copy-start(bf16[3,256,16,48]{1,3,2,0:T(8,128)(2,1)} %slice.131) | copy-start | bytes 3538948
  298.7 641.4 %all-reduce.10.cloned.1.call-start = ((), (), s32[]{:S(2)}) async-start(), calls=%async_computation.9 | async-start | bytes 16777216 | tf_op jit(solution)/shard_map/psum | solution.py:298
  354.3 94.2 %copy-start.39 = (bf16[3,256,16,64]{1,3,2,0:T(8,128)(2,1)S(1)}, bf16[3,256,16,64]{1,3,2,0:T(8,128)(2,1)}, u32[]{:S(2)}) copy-start(bf16[3,256,16,64]{1,3,2,0:T(8,128)(2,1)} %copy.77) | copy-start | bytes 4718596
  398.0 290.7 %copy-start.64 = (f32[3,16,1024]{2,1,0:T(8,128)}, f32[3,16,1024]{2,1,0:T(8,128)S(1)}, u32[]{:S(2)}) copy-start(f32[3,16,1024]{2,1,0:T(8,128)S(1)} %convert_element_type.203) | copy-start | bytes 589828
  500.9 63.8 %copy-start.13 = (bf16[3,256,16,48]{1,3,2,0:T(8,128)(2,1)S(1)}, bf16[3,256,16,48]{1,3,2,0:T(8,128)(2,1)}, u32[]{:S(2)}) copy-start(bf16[3,256,16,48]{1,3,2,0:T(8,128)(2,1)} %copy-done.12) | copy-start | bytes 3538948
  500.9 63.8 %copy-start.34 = (bf16[3,256,16,8]{1,3,2,0:T(8,128)(2,1)S(1)}, bf16[3,256,16,8]{1,3,2,0:T(8,128)(2,1)}, u32[]{:S(2)}) copy-start(bf16[3,256,16,8]{1,3,2,0:T(8,128)(2,1)} %copy-done.33) | copy-start | bytes 589828
  500.9 63.8 %copy-start.36 = (bf16[3,256,16,8]{1,3,2,0:T(8,128)(2,1)S(1)}, bf16[3,256,16,8]{1,3,2,0:T(8,128)(2,1)}, u32[]{:S(2)}) copy-start(bf16[3,256,16,8]{1,3,2,0:T(8,128)(2,1)} %copy-done.35) | copy-start | bytes 589828
  586.7 102.0 %copy-start.60 = (pred[1024,256]{1,0:T(8,128)(4,1)S(1)}, pred[1024,256]{1,0:T(8,128)(4,1)}, u32[]{:S(2)}) copy-start(pred[1024,256]{1,0:T(8,128)(4,1)} %iota_compare_fusion) | copy-start | bytes 786436
  709.2 28.0 %copy-start.15 = (f32[3,256,16,64]{1,3,2,0:T(8,128)S(1)}, f32[3,256,16,64]{1,3,2,0:T(8,128)}, u32[]{:S(2)}) copy-start(f32[3,256,16,64]{1,3,2,0:T(8,128)} %multiply_bitcast_fusion.1) | copy-start | bytes 9437188
  709.2 28.0 %copy-start.67 = (f32[256,8]{0,1:T(8,128)S(1)}, f32[256,8]{0,1:T(8,128)}, u32[]{:S(2)}) copy-start(f32[256,8]{0,1:T(8,128)} %copy-done.66) | copy-start | bytes 24580
  709.2 28.0 %copy-start.69 = (f32[256,8]{0,1:T(8,128)S(1)}, f32[256,8]{0,1:T(8,128)}, u32[]{:S(2)}) copy-start(f32[256,8]{0,1:T(8,128)} %copy-done.68) | copy-start | bytes 24580
  761.6 215.2 %all-gather.26.cloned.1.call-start = ((), (), s32[]{:S(2)}) async-start(), calls=%async_computation.8 | async-start | bytes 2359296 | tf_op jit(solution)/shard_map/all_gather | solution.py:321
  772.8 13.2 %copy-start.3 = (f32[768,1024]{1,0:T(8,128)}, f32[768,1024]{1,0:T(8,128)S(1)}, u32[]{:S(2)}) copy-start(f32[768,1024]{1,0:T(8,128)S(1)} %convolution_add_fusion) | copy-start | bytes 9437188
  836.6 106.2 %copy-start.41 = (bf16[128,1024]{1,0:T(8,128)(2,1)S(1)}, bf16[128,1024]{1,0:T(8,128)(2,1)}, u32[]{:S(2)}) copy-start(bf16[128,1024]{1,0:T(8,128)(2,1)} %copy-done.40) | copy-start | bytes 786436
  836.6 106.2 %copy-start.53 = (bf16[768,128]{1,0:T(8,128)(2,1)S(1)}, bf16[768,128]{1,0:T(8,128)(2,1)}, u32[]{:S(2)}) copy-start(bf16[768,128]{1,0:T(8,128)(2,1)} %copy-done.52) | copy-start | bytes 589828
  836.6 106.2 %copy-start.82 = (f32[1024]{0:T(1024)S(1)}, f32[1024]{0:T(1024)}, u32[]{:S(2)}) copy-start(f32[1024]{0:T(1024)} %convert_element_type.191) | copy-start | bytes 12292
  836.6 106.2 %copy-start.83 = (f32[1024]{0:T(1024)S(1)}, f32[1024]{0:T(1024)}, u32[]{:S(2)}) copy-start(f32[1024]{0:T(1024)} %slice_convert_fusion.2) | copy-start | bytes 12292
  942.8 29.6 %copy-start.30 = (f32[128,1024]{1,0:T(8,128)}, f32[128,1024]{1,0:T(8,128)S(1)}, u32[]{:S(2)}) copy-start(f32[128,1024]{1,0:T(8,128)S(1)} %get-tuple-element.93) | copy-start | bytes 1572868
  952.5 16.4 %copy-start.43 = (s32[512,128]{1,0:T(8,128)S(1)}, s32[512,128]{1,0:T(8,128)}, u32[]{:S(2)}) copy-start(s32[512,128]{1,0:T(8,128)} %param.49) | copy-start | bytes 786436
  952.5 16.4 %copy-start.57 = (f32[512,128]{1,0:T(8,128)S(1)}, f32[512,128]{1,0:T(8,128)}, u32[]{:S(2)}) copy-start(f32[512,128]{1,0:T(8,128)} %param.45) | copy-start | bytes 786436
  953.7 18.7 %copy-start.27 = (f32[128,1024]{1,0:T(8,128)S(1)}, f32[128,1024]{1,0:T(8,128)}, u32[]{:S(2)}) copy-start(f32[128,1024]{1,0:T(8,128)} %param.42) | copy-start | bytes 1572868
  953.7 18.7 %copy-start.28 = (f32[128,1024]{1,0:T(8,128)S(1)}, f32[128,1024]{1,0:T(8,128)}, u32[]{:S(2)}) copy-start(f32[128,1024]{1,0:T(8,128)} %param.46) | copy-start | bytes 1572868
  957.2 19.6 %copy-start.63 = (f32[128,128]{1,0:T(8,128)}, f32[128,128]{1,0:T(8,128)S(1)}, u32[]{:S(2)}) copy-start(f32[128,128]{1,0:T(8,128)S(1)} %get-tuple-element.89) | copy-start | bytes 196612
  957.2 17.4 %copy-start.42 = (bf16[512,1024]{1,0:T(8,128)(2,1)S(1)}, bf16[512,1024]{1,0:T(8,128)(2,1)}, u32[]{:S(2)}) copy-start(bf16[512,1024]{1,0:T(8,128)(2,1)} %param.32) | copy-start | bytes 3145732
  957.2 17.4 %copy-start.59 = (f32[512,128]{1,0:T(8,128)S(1)}, f32[512,128]{1,0:T(8,128)}, u32[]{:S(2)}) copy-start(f32[512,128]{1,0:T(8,128)} %param.37) | copy-start | bytes 786436
  957.2 17.4 %copy-start.62 = (f32[512,128]{1,0:T(8,128)S(1)}, f32[512,128]{1,0:T(8,128)}, u32[]{:S(2)}) copy-start(f32[512,128]{1,0:T(8,128)} %param.41) | copy-start | bytes 786436
  (57 other events, 264.2 us)
Sparse Core Ops, SparseCore 0:
  9.9 92.5 all-gather.9
  105.0 27.8 all-gather.11
  134.8 55.4 all-gather.17
  192.6 23.4 all-gather.19
  217.6 114.8 all-gather.15
  333.9 114.6 all-gather.13
  450.1 114.6 all-gather.21
  566.3 113.7 all-gather.23
  761.7 178.4 all-reduce.9
  942.9 28.6 all-gather.25
where the time goes:
time: 999 us; the launch traced here: 990 us
  waiting for transfers between devices  400 us (40%)
  matrix products  326 us (33%)
  blocking collectives  121 us (12%)
  other arithmetic  68.4 us (7%)
  local copies, waits for them, and re-layouts  58.5 us (6%)
  between operations  15.7 us (2%)
    psum x1, waiting for transfers between devices, body(): lax.psum((grad_a_part, grad_a_ffp, grad_b_part, grad_b_ffp, gain_part, sh...  104 us
    all_gather x1, waiting for transfers between devices, body(): lax.all_gather(grad_att.reshape(seqs, span, width), 'blk', axis=1, tiled=...  93.3 us
    dot_general x12, matrix products, matrix_product(): return jnp.dot(left, right, preferred_element_type=jnp.float32)  91.1 us
    dot_general x12, matrix products, product_right_transposed(): lax.dot_general(left, right, (((1,), (1,)), ((), ())), preferred_element_...  72.7 us
    all_gather x1, waiting for transfers between devices, body(): lax.all_gather(shards[0], 'dp', axis=0, tiled=True)  72.5 us
    all_gather x1, waiting for transfers between devices, body(): value_piece = lax.all_gather(value_send, 'blk', axis=1, tiled=True)  50.5 us
    psum x1, blocking collectives, body(): lax.psum((grad_a_part, grad_a_ffp, grad_b_part, grad_b_ffp, gain_part, sh...  39.3 us
    all_gather x1, waiting for transfers between devices, body(): lax.all_gather(query_b.reshape(seqs, span, width), 'blk', axis=1, tiled=T...  35.5 us
  transfers between devices with their start and end apart: 10, of which 8 were waited for; matrix products, arithmetic and copies ran while one was open for 36% of the time, Pallas kernels for 0%

commit v1 on v0

--- a/solution.py
+++ b/solution.py
@@ -3,6 +3,7 @@
 import jax.numpy as jnp
 from jax import lax
 from jax.sharding import PartitionSpec as P
+from jax.lax import all_gather
 
 HEADS = 16
 ROTARY = 16
@@ -144,6 +145,14 @@
     keep_b,
     keep_b_ff,
 ):
+
+    def settle_core(content, vector):
+        return jnp.split(
+            all_gather(jnp.concatenate([content, vector], 0), "blk", axis=1, tiled=True),
+            [content.shape[0]],
+            0,
+        )
+
     seqs, span, width = tokens.shape
     rows = seqs * span
     rank = adapt_b.shape[0]
@@ -190,8 +199,7 @@
     key_send = key_local.reshape(seqs, span, width)
     value_send = value_local.reshape(seqs, span, width)
     top = jnp.full((seqs, HEADS, span), masked_score, jnp.float32)
-    key_piece = lax.all_gather(key_send, "blk", axis=1, tiled=True)
-    value_piece = lax.all_gather(value_send, "blk", axis=1, tiled=True)
+    key_piece, value_piece = settle_core(key_send, value_send)
     count = key_piece.shape[1]
     key_h = key_piece.reshape(seqs, count, HEADS, depth)
     value_h = value_piece.reshape(seqs, count, HEADS, depth)

time: 999 us -> 1240 us (1.24)
  waiting for transfers between devices: 400 us -> 610 us
  matrix products: 326 us -> 351 us
  local copies, waits for them, and re-layouts: 58.5 us -> 70.9 us
    all_gather x0 -> x1, waiting for transfers between devices: none -> 209 us  [settle_core(): all_gather(jnp.concatenate([content, vector], 0), 'blk', axis=1, tiled=True)]
    all_gather x1, waiting for transfers between devices: 21.1 us -> 92.7 us  [body(): key_piece = lax.all_gather(key_send, 'blk', axis=1, tiled=True)]
    all_gather x1, waiting for transfers between devices: 50.5 us -> 0.01 us  [body(): value_piece = lax.all_gather(value_send, 'blk', axis=1, tiled=True)]
    dot_general x1 -> x2, matrix products: 21.8 us -> 42.6 us  [body(): jnp.einsum('sqhe,skhe->shqk', query_b, key_h, preferred_element_type=jnp....]
    all_gather x1, waiting for transfers between devices: 35.5 us -> 16.6 us  [body(): lax.all_gather(query_b.reshape(seqs, span, width), 'blk', axis=1, tiled=T...]
  transfers between devices with their start and end apart: 10 -> 11, of which waited for: 8 -> 7; matrix products, arithmetic and copies ran while one was open for 36% -> 34% of each run, Pallas kernels for 0% -> 0%
where the time goes in v1:
time: 1240 us; the launch traced here: 1230 us
  waiting for transfers between devices  610 us (49%)
  matrix products  351 us (28%)
  blocking collectives  118 us (10%)
  local copies, waits for them, and re-layouts  70.9 us (6%)
  other arithmetic  66.4 us (5%)
  between operations  15.7 us (1%)
    all_gather x1, waiting for transfers between devices, settle_core(): all_gather(jnp.concatenate([content, vector], 0), 'blk', axis=1, tiled=True)  209 us
    psum x1, waiting for transfers between devices, body(): lax.psum((grad_a_part, grad_a_ffp, grad_b_part, grad_b_ffp, gain_part, sh...  104 us
    all_gather x1, waiting for transfers between devices, body(): key_piece = lax.all_gather(key_send, 'blk', axis=1, tiled=True)  92.7 us
    all_gather x1, waiting for transfers between devices, body(): lax.all_gather(grad_att.reshape(seqs, span, width), 'blk', axis=1, tiled=...  92 us
    dot_general x12, matrix products, matrix_product(): return jnp.dot(left, right, preferred_element_type=jnp.float32)  91.7 us
    all_gather x1, waiting for transfers between devices, body(): lax.all_gather(shards[0], 'dp', axis=0, tiled=True)  74.9 us
    dot_general x12, matrix products, product_right_transposed(): lax.dot_general(left, right, (((1,), (1,)), ((), ())), preferred_element_...  74.3 us
    dot_general x2, matrix products, body(): jnp.einsum('sqhe,skhe->shqk', query_b, key_h, preferred_element_type=jnp....  42.6 us
  transfers between devices with their start and end apart: 11, of which 7 were waited for; matrix products, arithmetic and copies ran while one was open for 34% of the time, Pallas kernels for 0%

profile of v1, /device:TPU:0, one launch (start us, length us, event | category | flops | bytes accessed | tf_op | source)
XLA Modules:
  0.0 1233.2 jit_solution(7462082447765560982)
XLA Ops:
  12.9 11.8 all_gather.46
  27.6 74.9 %all-gather.11.cloned.1.call-done = bf16[1024,8192]{1,0:T(8,128)(2,1)} async-done(((bf16[128,8192]{1,0:T(8,128)(2,1)}), bf16[1024,8192]{1,0:T(8,128)(2,1)}) %all-gather.11.cloned.1.call-update) | async-done | bytes 16777232 | tf_op jit(solution)/shard_map/all_gather | solution.py:170
  102.5 10.2 fusion.24
  112.7 20.2 %all-gather.13.cloned.1.call-done = bf16[128,8192]{1,0:T(8,128)(2,1)} async-done(((bf16[128,1024]{1,0:T(8,128)(2,1)}), bf16[128,8192]{1,0:T(8,128)(2,1)}) %all-gather.13.cloned.1.call-update) | async-done | bytes 2097168 | tf_op jit(solution)/shard_map/all_gather | solution.py:174
  132.9 5.4 multiply_add_fusion.1
  138.3 2.8 fusion.133
  147.3 4.0 copy.74
  161.4 3.7 fusion.58
  167.8 3.3 slice.131
  172.9 4.0 pad_maximum_fusion.1
  183.7 9.1 all_gather.51
  197.4 12.8 %fusion.139 = f32[768,4096]{1,0:T(8,128)} fusion(bf16[768,1024]{1,0:T(8,128)(2,1)S(1)} %fusion.29, bf16[4096,1024]{1,0:T(8,128)(2,1)} %all-gather.17.cloned.1.call-done), kind=kOutput, calls=%fused_computation.236 | convolution fusion | flops 6442450944 | bytes 22544384 | tf_op jit(solution)/shard_map/dot_general | solution.py:25
  210.1 3.3 reshape.297
  213.4 5.1 copy.79
  218.5 9.2 fusion.20
  227.8 31.8 %multiply_convert_fusion.2 = (bf16[768,4096]{1,0:T(8,128)(2,1)}, f32[768,4096]{1,0:T(8,128)}, f32[768,4096]{1,0:T(8,128)}) fusion(bf16[768,128]{1,0:T(8,128)(2,1)S(1)} %convolution_convert_fusion.1, bf16[128,8192]{1,0:T(8,128)(2,1)S(1)} %copy-done.61, f32[768,4096]{1,0:T(8,128)S(1)} %fusion.20, f32[4096]{0:T(1024)S(1)} %slice_convert_fusion), kind=kOutput, calls=%fused_computation.16 | convolution fusion | flops 1019215872 | bytes 45301760 | tf_op jit(solution)/shard_map/dot_general | solution.py:21
  259.6 18.3 %add_convert_fusion = bf16[768,4096]{1,0:T(8,128)(2,1)} fusion(f32[768,4096]{1,0:T(8,128)} %get-tuple-element.99, f32[768,4096]{1,0:T(8,128)} %fusion.139, f32[768,4096]{1,0:T(8,128)} %get-tuple-element.138, bf16[768,128]{1,0:T(8,128)(2,1)S(1)} %fusion.70, bf16[4096,128]{1,0:T(8,128)(2,1)} %all-gather.19.cloned.1.call-done), kind=kOutput, calls=%fused_computation.15 | convolution fusion | flops 852492288 | bytes 45285376 | tf_op jit(solution)/shard_map/dot_general | solution.py:25
  277.9 5.0 fusion.71
  284.1 3.2 fusion.90
  289.8 6.1 fusion.143
  295.8 4.6 convolution_convert_fusion
  302.3 12.5 %fusion.138 = f32[768,1024]{1,0:T(8,128)} fusion(bf16[768,4096]{1,0:T(8,128)(2,1)} %get-tuple-element.98, bf16[4096,1024]{1,0:T(8,128)(2,1)} %all-gather.17.cloned.1.call-done), kind=kOutput, calls=%fused_computation.235 | convolution fusion | flops 6442450944 | bytes 17825792 | tf_op jit(solution)/shard_map/dot_general | solution.py:21
  314.8 16.6 %all-gather.25.cloned.1.call-done = bf16[3,1024,1024]{1,2,0:T(8,128)(2,1)} async-done(((bf16[3,256,1024]{1,2,0:T(8,128)(2,1)}), bf16[3,1024,1024]{1,2,0:T(8,128)(2,1)}) %all-gather.25.cloned.1.call-update) | async-done | bytes 6291472 | tf_op jit(solution)/shard_map/all_gather | solution.py:267
  331.4 21.8 %fusion.136 = f32[3,16,1024,256]{3,2,1,0:T(8,128)} fusion(bf16[3,1024,16,64]{1,3,2,0:T(8,128)(2,1)} %bitcast.182, bf16[3,256,16,48]{1,3,2,0:T(8,128)(2,1)S(1)} %copy-done.17, bf16[3,256,16,8]{1,3,2,0:T(8,128)(2,1)S(1)} %copy-done.42, bf16[3,256,16,8]{1,3,2,0:T(8,128)(2,1)S(1)} %copy-done.44), kind=kOutput, calls=%fused_computation.233 | convolution fusion | flops 1615331328 | bytes 58195968 | tf_op jit(solution)/shard_map/sqhe,skhe->shqk/dot_general | solution.py:273
  353.2 92.7 %all-gather.21.cloned.1.call-done = bf16[3,1024,1024]{1,2,0:T(8,128)(2,1)} async-done(((bf16[3,256,1024]{1,2,0:T(8,128)(2,1)}), bf16[3,1024,1024]{1,2,0:T(8,128)(2,1)}) %all-gather.21.cloned.1.call-update) | async-done | bytes 6291472 | tf_op jit(solution)/shard_map/all_gather | solution.py:245
  445.9 23.7 %fusion.137 = f32[3,16,256,1024]{3,2,1,0:T(8,128)} fusion(bf16[3,1024,16,64]{1,3,2,0:T(8,128)(2,1)} %bitcast.192, bf16[3,256,16,48]{1,3,2,0:T(8,128)(2,1)S(1)} %copy-done.6, bf16[3,256,16,8]{1,3,2,0:T(8,128)(2,1)S(1)} %copy-done.31, bf16[3,256,16,8]{1,3,2,0:T(8,128)(2,1)S(1)} %copy-done.29), kind=kOutput, calls=%fused_computation.234 | convolution fusion | flops 1615331328 | bytes 58195968 | tf_op jit(solution)/shard_map/sqhe,skhe->shqk/dot_general | solution.py:251
  469.6 92.0 %all-gather.27.cloned.1.call-done = bf16[3,1024,1024]{2,1,0:T(8,128)(2,1)} async-done(((bf16[3,256,1024]{2,1,0:T(8,128)(2,1)}), bf16[3,1024,1024]{2,1,0:T(8,128)(2,1)}) %all-gather.27.cloned.1.call-update) | async-done | bytes 6291472 | tf_op jit(solution)/shard_map/all_gather | solution.py:268
  561.6 8.8 copy.82
  570.4 208.7 %all-gather.15.cloned.1.call-done = bf16[6,1024,1024]{1,2,0:T(8,128)(2,1)} async-done(((bf16[6,256,1024]{1,2,0:T(8,128)(2,1)}), bf16[6,1024,1024]{1,2,0:T(8,128)(2,1)}) %all-gather.15.cloned.1.call-update) | async-done | bytes 12582928 | tf_op jit(solution)/shard_map/all_gather | solution.py:151
  779.1 8.6 fusion.132
  787.7 18.9 %fusion = (f32[3,16,256]{2,1,0:T(8,128)S(1)}, f32[3,16,256,1024]{3,2,1,0:T(8,128)}) fusion(pred[256,1024]{1,0:T(8,128)(4,1)S(1)} %copy-done.8, bf16[3,1024,16,64]{1,3,2,0:T(8,128)(2,1)S(1)} %bitcast.175, bf16[3,256,16,48]{1,3,2,0:T(8,128)(2,1)S(1)} %copy-done.6, bf16[3,256,16,8]{1,3,2,0:T(8,128)(2,1)S(1)} %copy-done.31, ...), kind=kOutput, calls=%fused_computation.5 | convolution fusion | flops 1653067776 | bytes 58507264 | tf_op jit(solution)/shard_map/sqhe,skhe->shqk/dot_general | solution.py:207
  806.6 23.3 %fusion.2 = f32[3,16,256]{2,1,0:T(8,128)S(1)} fusion(f32[3,16,256,1024]{3,2,1,0:T(8,128)} %get-tuple-element.137, f32[3,16,256]{2,1,0:T(8,128)S(1)} %broadcast_maximum_fusion, pred[256,1024]{1,0:T(8,128)(4,1)S(1)} %copy-done.8), kind=kLoop, calls=%fused_computation.7 | loop fusion | flops 62902272 | bytes 50692096 | tf_op jit(solution)/shard_map/reduce_sum | solution.py:214
  829.9 18.0 %all_gather.55 = bf16[3,16,1024]{2,1,0:T(8,128)(2,1)S(1)} all-gather(bf16[3,16,256]{2,1,0:T(8,128)(2,1)S(1)} %get-tuple-element.96), channel_id=1, replica_groups=mesh['dp'=8,'blk'=4] {'blk'}, dimensions={2}, use_global_device_ids=true | all-gather | bytes 122880 | tf_op jit(solution)/shard_map/all_gather | solution.py:262
  847.9 21.8 %multiply_reduce_fusion = (f32[3,256,16]{1,2,0:T(8,128)S(1)}, bf16[3,256,16,64]{1,3,2,0:T(8,128)(2,1)S(1)}) fusion(bf16[3,256,16,64]{1,3,2,0:T(8,128)(2,1)S(1)} %copy-done.46, f32[3,256,16]{1,2,0:T(8,128)S(1)} %bitcast.206, bf16[3,1024,16,64]{1,3,2,0:T(8,128)(2,1)} %bitcast.203, f32[3,16,256,1024]{3,2,1,0:T(8,128)} %get-tuple-element.137, ...), kind=kOutput, calls=%fused_computation.88 | convolution fusion | flops 1677447168 | bytes 60178432 | tf_op jit(solution)/shard_map/shqk,skhe->sqhe/dot_general | solution.py:215
  869.7 27.7 %all_gather.57 = bf16[3,16,1024]{2,1,0:T(8,128)(2,1)S(1)} all-gather(bf16[3,16,256]{2,1,0:T(8,128)(2,1)S(1)} %bitcast_convert_fusion), channel_id=1, replica_groups=mesh['dp'=8,'blk'=4] {'blk'}, dimensions={2}, use_global_device_ids=true | all-gather | bytes 122880 | tf_op jit(solution)/shard_map/all_gather | solution.py:265
  900.4 28.4 %multiply_bitcast_fusion = f32[3,256,16,64]{1,3,2,0:T(8,128)} fusion(bf16[3,1024,16,64]{1,3,2,0:T(8,128)(2,1)} %bitcast.183, f32[3,16,1024,256]{3,2,1,0:T(8,128)} %fusion.136, bf16[3,1024,16,64]{1,3,2,0:T(8,128)(2,1)} %bitcast.194, bf16[3,256,16,64]{1,3,2,0:T(8,128)(2,1)S(1)} %bitcast.178, f32[3,16,1024]{2,1,0:T(8,128)S(1)} %convert_element_type.206, ...), kind=kOutput, calls=%fused_computation.85 | convolution fusion | flops 3297509376 | bytes 68288512 | tf_op jit(solution)/shard_map/shqk,sqhe->skhe/dot_general | solution.py:284
  932.4 20.5 %fusion.65 = bf16[3,256,16,64]{1,3,2,0:T(8,128)(2,1)} fusion(bf16[3,1024,16,64]{1,3,2,0:T(8,128)(2,1)} %bitcast.195, f32[3,16,1024,256]{3,2,1,0:T(8,128)} %fusion.136, f32[3,16,1024]{2,1,0:T(8,128)S(1)} %convert_element_type.203, pred[1024,256]{1,0:T(8,128)(4,1)S(1)} %copy-done.65), kind=kOutput, calls=%fused_computation.99 | convolution fusion | flops 1661730816 | bytes 58654720 | tf_op jit(solution)/shard_map/shqk,sqhe->skhe/dot_general | solution.py:278
  952.9 29.6 %multiply_bitcast_fusion.1 = f32[3,256,16,64]{1,3,2,0:T(8,128)} fusion(bf16[3,1024,16,64]{1,3,2,0:T(8,128)(2,1)} %bitcast.193, f32[3,16,256,1024]{3,2,1,0:T(8,128)} %fusion.137, bf16[3,256,16,64]{1,3,2,0:T(8,128)(2,1)} %copy.79, bf16[3,1024,16,64]{1,3,2,0:T(8,128)(2,1)} %bitcast.222, f32[3,16,256]{2,1,0:T(8,128)S(1)} %bitcast.215, ...), kind=kOutput, calls=%fused_computation.87 | convolution fusion | flops 3297509376 | bytes 67993600 | tf_op jit(solution)/shard_map/shqk,skhe->sqhe/dot_general | solution.py:259
  1002.5 8.8 fusion.22
  1013.8 13.3 %fusion.129 = (f32[1024]{0:T(1024)S(1)}, f32[768]{0:T(1024)S(1)}, f32[768]{0:T(1024)S(1)}, f32[1024]{0:T(1024)S(1)}, f32[768,1024]{1,0:T(8,128)S(1)}) fusion(f32[1024]{0:T(1024)S(1)} %bitcast.212, f32[768]{0:T(1024)S(1)} %copy-done.75, bf16[3,256,1024]{2,1,0:T(8,128)(2,1)S(1)} %copy-done.1, f32[768,1024]{1,0:T(8,128)S(1)} %convolution_add_fusion, ...), kind=kOutput, calls=%fused_computation.227 | convolution fusion | flops 6451097600 | bytes 25715712 | tf_op jit(solution)/shard_map/dot_general | solution.py:25
  1027.2 2.9 fusion.45
  1030.2 41.3 %all-reduce.6 = (f32[2,1024]{1,0:T(2,128)}, f32[2,1024]{1,0:T(2,128)}) all-reduce(f32[2,1024]{1,0:T(2,128)S(1)} %pad_maximum_fusion.3, f32[2,1024]{1,0:T(2,128)S(1)} %pad_maximum_fusion.4), channel_id=1, replica_groups=mesh['dp'=8,'blk'=4] {'dp','blk'}, use_global_device_ids=true, to_apply=%region_12.13 | all-reduce | flops 4096 | bytes 32768 | tf_op jit(solution)/shard_map/psum | solution.py:306
  1071.4 3.1 fusion.94
  1074.6 5.1 fusion.60
  1079.7 103.6 %all-reduce.10.cloned.1.call-done = (f32[1024,384]{0,1:T(8,128)}, f32[4096,128]{1,0:T(8,128)}, f32[128,8192]{1,0:T(8,128)}, f32[128,1024]{1,0:T(8,128)}) async-done(((f32[1024,384]{0,1:T(8,128)}, f32[4096,128]{1,0:T(8,128)}, f32[128,8192]{1,0:T(8,128)}, f32[128,1024]{1,0:T(8,128)}), (f32[1024,384]{0,1:T(8,128)}, f32[4096,128]{1,0:T(8,128)}, f32[128,8192]{1,0:T(8,128)}, ...) | async-done | bytes 8388624 | tf_op jit(solution)/shard_map/psum | solution.py:306
  1186.0 6.1 fusion.52
  1192.4 3.2 fusion.31
  1200.3 10.0 all_gather.59
  (314 shorter events, 97.8 us)
Async XLA Ops:
  7.2 95.3 %all-gather.11.cloned.1.call-start = ((), (), s32[]{:S(2)}) async-start(), calls=%async_computation | async-start | bytes 18874368 | tf_op jit(solution)/shard_map/all_gather | solution.py:170
  8.0 125.0 %all-gather.13.cloned.1.call-start = ((), (), s32[]{:S(2)}) async-start(), calls=%async_computation.1 | async-start | bytes 2359296 | tf_op jit(solution)/shard_map/all_gather | solution.py:174
  9.9 187.5 %all-gather.17.cloned.1.call-start = ((), (), s32[]{:S(2)}) async-start(), calls=%async_computation.3 | async-start | bytes 9437184 | tf_op jit(solution)/shard_map/all_gather | solution.py:171
  10.6 249.0 %all-gather.19.cloned.1.call-start = ((), (), s32[]{:S(2)}) async-start(), calls=%async_computation.4 | async-start | bytes 1179648 | tf_op jit(solution)/shard_map/all_gather | solution.py:173
  11.4 320.0 %all-gather.25.cloned.1.call-start = ((), (), s32[]{:S(2)}) async-start(), calls=%async_computation.7 | async-start | bytes 7864320 | tf_op jit(solution)/shard_map/all_gather | solution.py:267
  11.7 15.2 %copy-start.74 = (f32[768]{0:T(1024)}, f32[768]{0:T(1024)S(1)}, u32[]{:S(2)}) copy-start(f32[768]{0:T(1024)S(1)} %div.87) | copy-start | bytes 9220
  12.4 14.6 %copy-start.76 = (f32[768]{0:T(1024)}, f32[768]{0:T(1024)S(1)}, u32[]{:S(2)}) copy-start(f32[768]{0:T(1024)S(1)} %rsqrt.13) | copy-start | bytes 9220
  12.4 14.6 %copy-start.78 = (f32[1,1024]{1,0:T(1,128)}, f32[1,1024]{1,0:T(1,128)S(1)}, u32[]{:S(2)}) copy-start(f32[1,1024]{1,0:T(1,128)S(1)} %get-tuple-element.128) | copy-start | bytes 12292
  12.4 14.6 %copy-start.80 = (f32[1,1024]{1,0:T(1,128)}, f32[1,1024]{1,0:T(1,128)S(1)}, u32[]{:S(2)}) copy-start(f32[1,1024]{1,0:T(1,128)S(1)} %get-tuple-element.129) | copy-start | bytes 12292
  24.9 126.5 %copy-start.70 = (f32[256,8]{0,1:T(8,128)}, f32[256,8]{0,1:T(8,128)S(1)}, u32[]{:S(2)}) copy-start(f32[256,8]{0,1:T(8,128)S(1)} %get-tuple-element.134) | copy-start | bytes 24580
  24.9 126.4 %copy-start.72 = (f32[256,8]{0,1:T(8,128)}, f32[256,8]{0,1:T(8,128)S(1)}, u32[]{:S(2)}) copy-start(f32[256,8]{0,1:T(8,128)S(1)} %get-tuple-element.135) | copy-start | bytes 24580
  27.0 85.8 %copy-start.24 = (bf16[768,1024]{1,0:T(8,128)(2,1)}, bf16[768,1024]{1,0:T(8,128)(2,1)S(1)}, u32[]{:S(2)}) copy-start(bf16[768,1024]{1,0:T(8,128)(2,1)S(1)} %get-tuple-element.114) | copy-start | bytes 4718596
  27.6 105.4 %copy-start.52 = (bf16[768,128]{1,0:T(8,128)(2,1)}, bf16[768,128]{1,0:T(8,128)(2,1)S(1)}, u32[]{:S(2)}) copy-start(bf16[768,128]{1,0:T(8,128)(2,1)S(1)} %convolution_convert_fusion.3) | copy-start | bytes 589828
  154.5 291.4 %all-gather.21.cloned.1.call-start = ((), (), s32[]{:S(2)}) async-start(), calls=%async_computation.5 | async-start | bytes 7864320 | tf_op jit(solution)/shard_map/all_gather | solution.py:245
  158.9 402.7 %all-gather.27.cloned.1.call-start = ((), (), s32[]{:S(2)}) async-start(), calls=%async_computation.8 | async-start | bytes 7864320 | tf_op jit(solution)/shard_map/all_gather | solution.py:268
  159.6 140.8 %copy-start.9 = (bf16[768,1024]{1,0:T(8,128)(2,1)}, bf16[768,1024]{1,0:T(8,128)(2,1)S(1)}, u32[]{:S(2)}) copy-start(bf16[768,1024]{1,0:T(8,128)(2,1)S(1)} %fusion.29) | copy-start | bytes 4718596
  167.8 611.3 %all-gather.15.cloned.1.call-start = ((), (), s32[]{:S(2)}) async-start(), calls=%async_computation.2 | async-start | bytes 15728640 | tf_op jit(solution)/shard_map/all_gather | solution.py:151
  176.9 18.9 %copy-start.26 = (bf16[768,1024]{1,0:T(8,128)(2,1)S(1)}, bf16[768,1024]{1,0:T(8,128)(2,1)}, u32[]{:S(2)}) copy-start(bf16[768,1024]{1,0:T(8,128)(2,1)} %get-tuple-element.115) | copy-start | bytes 4718596
  177.0 776.0 %all-gather.23.cloned.1.call-start = ((), (), s32[]{:S(2)}) async-start(), calls=%async_computation.6 | async-start | bytes 7864320 | tf_op jit(solution)/shard_map/all_gather | solution.py:246
  197.3 12.8 %copy-start.13 = (bf16[768,1024]{1,0:T(8,128)(2,1)S(1)}, bf16[768,1024]{1,0:T(8,128)(2,1)}, u32[]{:S(2)}) copy-start(bf16[768,1024]{1,0:T(8,128)(2,1)} %add_convert_fusion.3) | copy-start | bytes 4718596
  289.7 893.6 %all-reduce.10.cloned.1.call-start = ((), (), s32[]{:S(2)}) async-start(), calls=%async_computation.10 | async-start | bytes 16777216 | tf_op jit(solution)/shard_map/psum | solution.py:306
  302.3 29.1 %copy-start.17 = (bf16[3,256,16,48]{1,3,2,0:T(8,128)(2,1)S(1)}, bf16[3,256,16,48]{1,3,2,0:T(8,128)(2,1)}, u32[]{:S(2)}) copy-start(bf16[3,256,16,48]{1,3,2,0:T(8,128)(2,1)} %copy-done.16) | copy-start | bytes 3538948
  302.3 29.1 %copy-start.42 = (bf16[3,256,16,8]{1,3,2,0:T(8,128)(2,1)S(1)}, bf16[3,256,16,8]{1,3,2,0:T(8,128)(2,1)}, u32[]{:S(2)}) copy-start(bf16[3,256,16,8]{1,3,2,0:T(8,128)(2,1)} %copy-done.41) | copy-start | bytes 589828
  302.3 29.1 %copy-start.44 = (bf16[3,256,16,8]{1,3,2,0:T(8,128)(2,1)S(1)}, bf16[3,256,16,8]{1,3,2,0:T(8,128)(2,1)}, u32[]{:S(2)}) copy-start(bf16[3,256,16,8]{1,3,2,0:T(8,128)(2,1)} %copy-done.43) | copy-start | bytes 589828
  331.4 114.5 %copy-start.6 = (bf16[3,256,16,48]{1,3,2,0:T(8,128)(2,1)S(1)}, bf16[3,256,16,48]{1,3,2,0:T(8,128)(2,1)}, u32[]{:S(2)}) copy-start(bf16[3,256,16,48]{1,3,2,0:T(8,128)(2,1)} %copy-done.5) | copy-start | bytes 3538948
  331.4 114.5 %copy-start.29 = (bf16[3,256,16,8]{1,3,2,0:T(8,128)(2,1)S(1)}, bf16[3,256,16,8]{1,3,2,0:T(8,128)(2,1)}, u32[]{:S(2)}) copy-start(bf16[3,256,16,8]{1,3,2,0:T(8,128)(2,1)} %copy-done.28) | copy-start | bytes 589828
  331.4 114.5 %copy-start.31 = (bf16[3,256,16,8]{1,3,2,0:T(8,128)(2,1)S(1)}, bf16[3,256,16,8]{1,3,2,0:T(8,128)(2,1)}, u32[]{:S(2)}) copy-start(bf16[3,256,16,8]{1,3,2,0:T(8,128)(2,1)} %copy-done.30) | copy-start | bytes 589828
  570.4 217.3 %copy-start.8 = (pred[256,1024]{1,0:T(8,128)(4,1)S(1)}, pred[256,1024]{1,0:T(8,128)(4,1)}, u32[]{:S(2)}) copy-start(pred[256,1024]{1,0:T(8,128)(4,1)} %iota_compare_fusion.1) | copy-start | bytes 786436
  806.6 41.4 %copy-start.46 = (bf16[3,256,16,64]{1,3,2,0:T(8,128)(2,1)S(1)}, bf16[3,256,16,64]{1,3,2,0:T(8,128)(2,1)}, u32[]{:S(2)}) copy-start(bf16[3,256,16,64]{1,3,2,0:T(8,128)(2,1)} %copy.79) | copy-start | bytes 4718596
  952.9 29.6 %copy-start.71 = (f32[256,8]{0,1:T(8,128)S(1)}, f32[256,8]{0,1:T(8,128)}, u32[]{:S(2)}) copy-start(f32[256,8]{0,1:T(8,128)} %copy-done.70) | copy-start | bytes 24580
  952.9 29.6 %copy-start.73 = (f32[256,8]{0,1:T(8,128)S(1)}, f32[256,8]{0,1:T(8,128)}, u32[]{:S(2)}) copy-start(f32[256,8]{0,1:T(8,128)} %copy-done.72) | copy-start | bytes 24580
  1002.4 217.4 %all-gather.29.cloned.1.call-start = ((), (), s32[]{:S(2)}) async-start(), calls=%async_computation.9 | async-start | bytes 2359296 | tf_op jit(solution)/shard_map/all_gather | solution.py:329
  1013.8 13.4 %copy-start.3 = (f32[768,1024]{1,0:T(8,128)}, f32[768,1024]{1,0:T(8,128)S(1)}, u32[]{:S(2)}) copy-start(f32[768,1024]{1,0:T(8,128)S(1)} %convolution_add_fusion) | copy-start | bytes 9437188
  1013.8 13.3 %copy-start.85 = (f32[768]{0:T(1024)S(1)}, f32[768]{0:T(1024)}, u32[]{:S(2)}) copy-start(f32[768]{0:T(1024)} %copy-done.84) | copy-start | bytes 9220
  1013.8 13.4 %copy-start.77 = (f32[768]{0:T(1024)S(1)}, f32[768]{0:T(1024)}, u32[]{:S(2)}) copy-start(f32[768]{0:T(1024)} %copy-done.76) | copy-start | bytes 9220
  1079.7 106.2 %copy-start.48 = (bf16[128,1024]{1,0:T(8,128)(2,1)S(1)}, bf16[128,1024]{1,0:T(8,128)(2,1)}, u32[]{:S(2)}) copy-start(bf16[128,1024]{1,0:T(8,128)(2,1)} %copy-done.47) | copy-start | bytes 786436
  1079.7 106.2 %copy-start.60 = (bf16[768,128]{1,0:T(8,128)(2,1)S(1)}, bf16[768,128]{1,0:T(8,128)(2,1)}, u32[]{:S(2)}) copy-start(bf16[768,128]{1,0:T(8,128)(2,1)} %copy-done.59) | copy-start | bytes 589828
  1079.7 106.2 %copy-start.86 = (f32[1024]{0:T(1024)S(1)}, f32[1024]{0:T(1024)}, u32[]{:S(2)}) copy-start(f32[1024]{0:T(1024)} %convert_element_type.191) | copy-start | bytes 12292
  1079.7 106.2 %copy-start.87 = (f32[1024]{0:T(1024)S(1)}, f32[1024]{0:T(1024)}, u32[]{:S(2)}) copy-start(f32[1024]{0:T(1024)} %slice_convert_fusion.2) | copy-start | bytes 12292
  1185.8 29.6 %copy-start.38 = (f32[128,1024]{1,0:T(8,128)}, f32[128,1024]{1,0:T(8,128)S(1)}, u32[]{:S(2)}) copy-start(f32[128,1024]{1,0:T(8,128)S(1)} %get-tuple-element.93) | copy-start | bytes 1572868
  1195.6 16.3 %copy-start.50 = (s32[512,128]{1,0:T(8,128)S(1)}, s32[512,128]{1,0:T(8,128)}, u32[]{:S(2)}) copy-start(s32[512,128]{1,0:T(8,128)} %param.49) | copy-start | bytes 786436
  1195.6 16.3 %copy-start.62 = (f32[512,128]{1,0:T(8,128)S(1)}, f32[512,128]{1,0:T(8,128)}, u32[]{:S(2)}) copy-start(f32[512,128]{1,0:T(8,128)} %param.45) | copy-start | bytes 786436
  1196.8 18.7 %copy-start.35 = (f32[128,1024]{1,0:T(8,128)S(1)}, f32[128,1024]{1,0:T(8,128)}, u32[]{:S(2)}) copy-start(f32[128,1024]{1,0:T(8,128)} %param.42) | copy-start | bytes 1572868
  1196.8 18.7 %copy-start.36 = (f32[128,1024]{1,0:T(8,128)S(1)}, f32[128,1024]{1,0:T(8,128)}, u32[]{:S(2)}) copy-start(f32[128,1024]{1,0:T(8,128)} %param.46) | copy-start | bytes 1572868
  1200.2 19.5 %copy-start.69 = (f32[128,128]{1,0:T(8,128)}, f32[128,128]{1,0:T(8,128)S(1)}, u32[]{:S(2)}) copy-start(f32[128,128]{1,0:T(8,128)S(1)} %get-tuple-element.89) | copy-start | bytes 196612
  1200.3 17.4 %copy-start.49 = (bf16[512,1024]{1,0:T(8,128)(2,1)S(1)}, bf16[512,1024]{1,0:T(8,128)(2,1)}, u32[]{:S(2)}) copy-start(bf16[512,1024]{1,0:T(8,128)(2,1)} %param.32) | copy-start | bytes 3145732
  1200.3 17.4 %copy-start.64 = (f32[512,128]{1,0:T(8,128)S(1)}, f32[512,128]{1,0:T(8,128)}, u32[]{:S(2)}) copy-start(f32[512,128]{1,0:T(8,128)} %param.37) | copy-start | bytes 786436
  1200.3 17.4 %copy-start.68 = (f32[512,128]{1,0:T(8,128)S(1)}, f32[512,128]{1,0:T(8,128)}, u32[]{:S(2)}) copy-start(f32[512,128]{1,0:T(8,128)} %param.41) | copy-start | bytes 786436
  (60 other events, 214.3 us)
Sparse Core Ops, SparseCore 0:
  9.9 92.5 all-gather.10
  105.0 27.8 all-gather.12
  134.8 54.3 all-gather.16
  191.6 23.4 all-gather.18
  216.5 114.8 all-gather.24
  332.8 113.0 all-gather.20
  448.0 113.5 all-gather.26
  563.2 215.8 all-gather.14
  780.6 116.2 all-gather.22
  1002.6 180.6 all-reduce.9
  1186.0 28.6 all-gather.28
